TPU v7x, 32 devices: a whole 2x2x4 slice. The times are simulated.
32 devices in a mesh: dp: 8 (over z, core), tensor: 4 (over y, x).
Axes of the slice: x: 2, y: 2, z: 4, core: 2. Of those that a mesh axis runs over, the one named last changes fastest.
Arguments:
- block_input: bfloat16 [8192, 2048], P(('dp', 'tensor')), may hold values from -60 to 60
- norm_gain: float32 [2048], replicated, may hold values from 0.5 to 1.5
- norm_shift: float32 [2048], replicated, may hold values from -1.8 to 1.8
- qkv_weight: bfloat16 [3, 2048, 2048], P(None, None, 'tensor'), may hold values from -1 to 1
- qkv_bias: float32 [3, 2048], P(None, 'tensor'), may hold values from -1.8 to 1.8
- dense_weight: bfloat16 [2048, 2048], P('tensor'), may hold values from -1.5 to 1.5
- dense_bias: float32 [2048], replicated, may hold values from -1.8 to 1.8
- fc1_weight: bfloat16 [2048, 8192], P(None, 'tensor'), may hold values from -0.125 to 0.125
- fc1_bias: float32 [8192], P('tensor'), may hold values from -1.8 to 1.8
- fc2_weight: bfloat16 [8192, 2048], P('tensor'), may hold values from -0.0625 to 0.0625
- fc2_bias: float32 [2048], replicated, may hold values from -1.8 to 1.8
- cotangent: bfloat16 [8192, 2048], P(('dp', 'tensor')), may hold values from -6 to 6
Outputs:
- block_output: bfloat16 [8192, 2048], P(('dp', 'tensor'))
- input_grad: float32 [8192, 2048], P(('dp', 'tensor'))
- grad_norm_gain: float32 [2048], replicated
- grad_norm_shift: float32 [2048], replicated
- grad_qkv_weight: float32 [3, 2048, 2048], P(None, None, 'tensor')
- grad_qkv_bias: float32 [3, 2048], P(None, 'tensor')
- grad_dense_weight: float32 [2048, 2048], P('tensor')
- grad_dense_bias: float32 [2048], replicated
- grad_fc1_weight: float32 [2048, 8192], P(None, 'tensor')
- grad_fc1_bias: float32 [8192], P('tensor')
- grad_fc2_weight: float32 [8192, 2048], P('tensor')
- grad_fc2_bias: float32 [2048], replicated
All inputs are finite; a program needn't handle non-finite values.
Results may differ from a plain program's by a relative error of at most 0.0099.
Values may be sent and summed in bfloat16 or wider, within the bound.
No kernel may reach another device: no remote copies, remote signals or barrier semaphores. Data moves between devices by JAX's collectives and lax.ppermute only.
A program may use at most 320 MiB of HBM per device.

v0:
```python
import math
import jax
import jax.numpy as jnp
from jax import lax
from jax.sharding import PartitionSpec as P

HD = 64
ROT = 32
norm_eps = 1e-05
gelu_scale = math.sqrt(2.0 / math.pi)
gelu_cubic = 0.044715
masked_value = -1e30


def rope_tables(length):
    halfway = ROT // 2
    inverse = 10000.0 ** (-(2.0 * jnp.arange(halfway, dtype=jnp.float32)) / ROT)
    angles = jnp.arange(length, dtype=jnp.float32)[:, None] * inverse[None, :]
    angles = jnp.concatenate([angles, angles], axis=1)
    return (jnp.cos(angles), jnp.sin(angles))


def rotate(inputs, cosine_table, sine_table):
    halfway = ROT // 2
    rotary = inputs[..., :ROT]
    turned = jnp.concatenate([-rotary[..., halfway:], rotary[..., :halfway]], axis=-1)
    mixed = rotary * cosine_table[:, None, :] + turned * sine_table[:, None, :]
    return jnp.concatenate([mixed, inputs[..., ROT:]], axis=-1)


def rotate_back(grads, cosine_table, sine_table):
    halfway = ROT // 2
    rotary = grads[..., :ROT]
    scaled = rotary * sine_table[:, None, :]
    turned = jnp.concatenate([scaled[..., halfway:], -scaled[..., :halfway]], axis=-1)
    mixed = rotary * cosine_table[:, None, :] + turned
    return jnp.concatenate([mixed, grads[..., ROT:]], axis=-1)


def gelu_parts(pre_act):
    inner = gelu_scale * (pre_act + gelu_cubic * pre_act * pre_act * pre_act)
    tangent = jnp.tanh(inner)
    value = 0.5 * pre_act * (1.0 + tangent)
    slope = 0.5 * (1.0 + tangent) + 0.5 * pre_act * (1.0 - tangent * tangent) * gelu_scale * (
        1.0 + 3.0 * gelu_cubic * pre_act * pre_act
    )
    return (value, slope)


def norm_forward(inputs, norm_gain, norm_shift):
    widened = inputs.astype(jnp.float32)
    row_mean = jnp.mean(widened, axis=-1, keepdims=True)
    centred = widened - row_mean
    variance = jnp.mean(centred * centred, axis=-1, keepdims=True)
    inv_std = lax.rsqrt(variance + norm_eps)
    normed = centred * inv_std
    return (normed, inv_std, (normed * norm_gain + norm_shift).astype(jnp.bfloat16))


def causal_scores(q_block, keys_all, offset):
    length = keys_all.shape[0]
    row_count = q_block.shape[0]
    scores = jnp.einsum(
        "qhd,khd->hqk", q_block, keys_all, preferred_element_type=jnp.float32
    ) * HD ** (-0.5)
    query_pos = offset + jnp.arange(row_count)
    key_pos = jnp.arange(length)
    allowed = key_pos[None, :] <= query_pos[:, None]
    return jnp.where(allowed[None], scores, masked_value)


def shards(
    block_input,
    norm_gain,
    norm_shift,
    qkv_weight,
    qkv_bias,
    dense_weight,
    dense_bias,
    fc1_weight,
    fc1_bias,
    fc2_weight,
    fc2_bias,
    cotangent,
):
    normed, inv_std, ln_local = norm_forward(block_input, norm_gain, norm_shift)
    ln_rows = lax.all_gather(ln_local, "tensor", axis=0, tiled=True)
    length = ln_rows.shape[0]
    local_width = qkv_weight.shape[2]
    head_count = local_width // HD
    cosine_table, sine_table = rope_tables(length)
    block_len = min(512, length)
    block_count = length // block_len
    projected = (
        jnp.einsum("td,jdc->jtc", ln_rows, qkv_weight, preferred_element_type=jnp.float32)
        + qkv_bias[:, None, :]
    )
    queries = rotate(projected[0].reshape(length, head_count, HD), cosine_table, sine_table).astype(
        jnp.bfloat16
    )
    keys_all = rotate(
        projected[1].reshape(length, head_count, HD), cosine_table, sine_table
    ).astype(jnp.bfloat16)
    values_all = projected[2].reshape(length, head_count, HD).astype(jnp.bfloat16)
    log_totals = []
    contexts = []
    for index in range(block_count):
        offset = index * block_len
        q_block = queries[offset : offset + block_len]
        scores = causal_scores(q_block, keys_all, offset)
        row_max = jnp.max(scores, axis=-1, keepdims=True)
        log_total = row_max + jnp.log(jnp.sum(jnp.exp(scores - row_max), axis=-1, keepdims=True))
        probs_b = jnp.exp(scores - log_total).astype(jnp.bfloat16)
        ctx_block = jnp.einsum(
            "hqk,khd->qhd", probs_b, values_all, preferred_element_type=jnp.float32
        )
        log_totals.append(log_total)
        contexts.append(ctx_block.astype(jnp.bfloat16))
    context = jnp.concatenate(contexts, axis=0).reshape(length, local_width)
    pre_act = jnp.dot(ln_rows, fc1_weight, preferred_element_type=jnp.float32) + fc1_bias
    act_value, act_slope = gelu_parts(pre_act)
    act_b = act_value.astype(jnp.bfloat16)
    partial_value = jnp.dot(context, dense_weight, preferred_element_type=jnp.float32) + jnp.dot(
        act_b, fc2_weight, preferred_element_type=jnp.float32
    )
    summed = lax.psum_scatter(partial_value, "tensor", scatter_dimension=0, tiled=True)
    block_output = (block_input.astype(jnp.float32) + summed + dense_bias + fc2_bias).astype(
        jnp.bfloat16
    )
    cot_rows = lax.all_gather(cotangent, "tensor", axis=0, tiled=True)
    grad_out_bias = jnp.sum(cot_rows.astype(jnp.float32), axis=0)
    grad_fc2_w = jnp.dot(act_b.T, cot_rows, preferred_element_type=jnp.float32)
    d_pre = jnp.dot(cot_rows, fc2_weight.T, preferred_element_type=jnp.float32) * act_slope
    grad_fc1_b = jnp.sum(d_pre, axis=0)
    d_pre_b = d_pre.astype(jnp.bfloat16)
    grad_fc1_w = jnp.dot(ln_rows.T, d_pre_b, preferred_element_type=jnp.float32)
    d_ln_mlp = jnp.dot(d_pre_b, fc1_weight.T, preferred_element_type=jnp.float32)
    grad_dense_w = jnp.dot(context.T, cot_rows, preferred_element_type=jnp.float32)
    d_context = (
        jnp.dot(cot_rows, dense_weight.T, preferred_element_type=jnp.float32)
        .astype(jnp.bfloat16)
        .reshape(length, head_count, HD)
    )
    d_keys = jnp.zeros((length, head_count, HD), jnp.float32)
    d_values = jnp.zeros((length, head_count, HD), jnp.float32)
    d_query_list = []
    for index in range(block_count):
        offset = index * block_len
        q_block = queries[offset : offset + block_len]
        scores = causal_scores(q_block, keys_all, offset)
        attn_probs = jnp.exp(scores - log_totals[index])
        probs_b = attn_probs.astype(jnp.bfloat16)
        grad_block = d_context[offset : offset + block_len]
        d_probs = jnp.einsum(
            "qhd,khd->hqk", grad_block, values_all, preferred_element_type=jnp.float32
        )
        row_dot = jnp.sum(attn_probs * d_probs, axis=-1, keepdims=True)
        d_scores = (attn_probs * (d_probs - row_dot) * HD ** (-0.5)).astype(jnp.bfloat16)
        d_query_list.append(
            jnp.einsum("hqk,khd->qhd", d_scores, keys_all, preferred_element_type=jnp.float32)
        )
        d_keys = d_keys + jnp.einsum(
            "hqk,qhd->khd", d_scores, q_block, preferred_element_type=jnp.float32
        )
        d_values = d_values + jnp.einsum(
            "hqk,qhd->khd", probs_b, grad_block, preferred_element_type=jnp.float32
        )
    d_queries = jnp.concatenate(d_query_list, axis=0)
    d_proj = jnp.stack(
        [
            rotate_back(d_queries, cosine_table, sine_table).reshape(length, local_width),
            rotate_back(d_keys, cosine_table, sine_table).reshape(length, local_width),
            d_values.reshape(length, local_width),
        ]
    )
    grad_qkv_b = jnp.sum(d_proj, axis=1)
    d_proj_b = d_proj.astype(jnp.bfloat16)
    grad_qkv_w = jnp.einsum("td,jtc->jdc", ln_rows, d_proj_b, preferred_element_type=jnp.float32)
    d_ln_part = d_ln_mlp + jnp.einsum(
        "jtc,jdc->td", d_proj_b, qkv_weight, preferred_element_type=jnp.float32
    )
    (
        grad_qkv_w,
        grad_qkv_b,
        grad_dense_w,
        grad_dense_b,
        grad_fc1_w,
        grad_fc1_b,
        grad_fc2_w,
        grad_fc2_b,
    ) = lax.psum(
        (
            grad_qkv_w,
            grad_qkv_b,
            grad_dense_w,
            grad_out_bias,
            grad_fc1_w,
            grad_fc1_b,
            grad_fc2_w,
            grad_out_bias,
        ),
        "dp",
    )
    d_ln = lax.psum_scatter(d_ln_part, "tensor", scatter_dimension=0, tiled=True)
    local_gain = jnp.sum(d_ln * normed, axis=0)
    local_shift = jnp.sum(d_ln, axis=0)
    d_normed = d_ln * norm_gain
    d_inputs = inv_std * (
        d_normed
        - jnp.mean(d_normed, axis=-1, keepdims=True)
        - normed * jnp.mean(d_normed * normed, axis=-1, keepdims=True)
    )
    input_grad = cotangent.astype(jnp.float32) + d_inputs
    grad_gain, grad_shift = lax.psum((local_gain, local_shift), ("dp", "tensor"))
    return (
        block_output,
        input_grad,
        grad_gain,
        grad_shift,
        grad_qkv_w,
        grad_qkv_b,
        grad_dense_w,
        grad_dense_b,
        grad_fc1_w,
        grad_fc1_b,
        grad_fc2_w,
        grad_fc2_b,
    )


def solution(mesh):
    placed = (
        P(("dp", "tensor"), None),
        P(),
        P(),
        P(None, None, "tensor"),
        P(None, "tensor"),
        P("tensor", None),
        P(),
        P(None, "tensor"),
        P("tensor"),
        P("tensor", None),
        P(),
        P(("dp", "tensor"), None),
    )
    return jax.shard_map(
        shards,
        mesh=mesh,
        in_specs=placed,
        out_specs=(
            P(("dp", "tensor"), None),
            P(("dp", "tensor"), None),
            P(),
            P(),
            P(None, None, "tensor"),
            P(None, "tensor"),
            P("tensor", None),
            P(),
            P(None, "tensor"),
            P("tensor"),
            P("tensor", None),
            P(),
        ),
        check_vma=False,
    )
```

profile of v0, /device:TPU:0, one launch (start us, length us, event | category | flops | bytes accessed | tf_op | source)
XLA Modules:
  0.0 1596.1 jit_solution(8423866442784530720)
XLA Ops:
  17.0 52.2 %all-gather.3.cloned.1.call-done = bf16[1024,2048]{1,0:T(8,128)(2,1)} async-done(((bf16[256,2048]{1,0:T(8,128)(2,1)}), bf16[1024,2048]{1,0:T(8,128)(2,1)}) %all-gather.3.cloned.1.call-update) | async-done | bytes 4194320 | tf_op jit(solution)/shard_map/all_gather | solution.py:87
  69.2 10.4 add_bitcast_fusion
  83.8 39.8 %all-gather.5.cloned.1.call-done = bf16[1024,2048]{1,0:T(8,128)(2,1)} async-done(((bf16[256,2048]{1,0:T(8,128)(2,1)}), bf16[1024,2048]{1,0:T(8,128)(2,1)}) %all-gather.5.cloned.1.call-update) | async-done | bytes 4194320 | tf_op jit(solution)/shard_map/all_gather | solution.py:130
  123.7 4.7 convolution_convert_fusion
  139.3 8.5 fusion.125
  147.8 37.9 %fusion.78 = f32[512,8,64]{0,2,1:T(8,128)} fusion(f32[8,512,1024]{2,1,0:T(8,128)} %fusion.125, bf16[1024,8,32]{0,2,1:T(8,128)(2,1)} %slice.176, bf16[1024,8,32]{0,2,1:T(8,128)(2,1)} %copy-done.30, f32[8,512,1024]{2,1,0:T(8,128)} %copy-done.3, f32[8,512]{1,0:T(8,128)S(1)} %log_add_fusion.1, pred[512,1024]{1,0:T(8,128)(4,1)} %iota_compare_fusion.2), kind=kOutput, calls=%fused_computation.92 | convolution fusion | flops 585110528 | bytes 36192256 | tf_op jit(solution)/shard_map/hqk,khd->qhd/dot_general | solution.py:160
  185.7 36.2 %fusion.11 = f32[8,64,1024]{2,1,0:T(8,128)} fusion(f32[8,512,1024]{2,1,0:T(8,128)} %fusion.125, bf16[1024,8,32]{0,2,1:T(8,128)(2,1)} %copy-done.28, bf16[1024,8,32]{0,2,1:T(8,128)(2,1)} %slice.177, f32[8,512,1024]{2,1,0:T(8,128)} %copy-done.3, f32[8,512]{1,0:T(8,128)S(1)} %log_add_fusion.1, pred[512,1024]{1,0:T(8,128)(4,1)} %iota_compare_fusion.2), kind=kOutput, calls=%fused_computation.18 | convolution fusion | flops 584061952 | bytes 71335936 | tf_op jit(solution)/shard_map/hqk,qhd->khd/dot_general | solution.py:162
  221.9 12.6 fusion.124
  234.6 20.6 %fusion.123 = (f32[2048]{0:T(1024)}, bf16[1024,2048]{1,0:T(8,128)(2,1)}) fusion(f32[1024,2048]{1,0:T(8,128)S(1)} %fusion.124, f32[2048]{0:T(1024)S(1)} %copy-done.50, bf16[1024,2048]{1,0:T(8,128)(2,1)S(1)} %copy-done.15, bf16[2048,2048]{1,0:T(8,128)(2,1)} %param.21), kind=kOutput, calls=%fused_computation.152 | convolution fusion | flops 8633972736 | bytes 25182208 | tf_op jit(solution)/shard_map/dot_general | solution.py:133
  255.2 15.1 fusion.68
  277.8 8.5 fusion.126
  290.9 9.8 fusion.72
  303.6 37.9 %fusion.75 = f32[512,8,64]{0,2,1:T(8,128)} fusion(f32[8,512,1024]{2,1,0:T(8,128)} %fusion.126, bf16[1024,8,32]{0,2,1:T(8,128)(2,1)} %slice.176, bf16[1024,8,32]{0,2,1:T(8,128)(2,1)} %copy-done.30, f32[8,512,1024]{2,1,0:T(8,128)} %copy-done.1, f32[8,512]{1,0:T(8,128)S(1)} %log_add_fusion, pred[512,1024]{1,0:T(8,128)(4,1)} %iota_compare_fusion.1), kind=kOutput, calls=%fused_computation.91 | convolution fusion | flops 585110528 | bytes 36192256 | tf_op jit(solution)/shard_map/hqk,khd->qhd/dot_general | solution.py:160
  341.5 36.2 %add_bitcast_fusion.1 = f32[1024,8,64]{0,2,1:T(8,128)} fusion(f32[8,64,1024]{2,1,0:T(8,128)} %fusion.11, f32[8,512,1024]{2,1,0:T(8,128)} %fusion.126, bf16[1024,8,32]{0,2,1:T(8,128)(2,1)} %slice.177, bf16[1024,8,32]{0,2,1:T(8,128)(2,1)} %copy-done.28, f32[8,512,1024]{2,1,0:T(8,128)} %copy-done.1, f32[8,512]{1,0:T(8,128)S(1)} %log_add_fusion, ...), kind=kOutput, calls=%fused_computation.81 | convolution fusion | flops 584586240 | bytes 39337984 | tf_op jit(solution)/shard_map/hqk,qhd->khd/dot_general | solution.py:162
  393.0 13.9 bitcast_add_fusion
  407.0 8.3 fusion.87
  415.3 8.3 fusion.90
  423.8 12.1 fusion.118
  435.8 5.6 convolution_add_fusion
  441.6 6.9 fusion.127
  448.5 10.3 convolution_bitcast_fusion
  458.8 11.8 fusion.66
  470.6 12.7 fusion.117
  488.1 29.0 %all-reduce.1 = (f32[3,512]{1,0:T(4,128)}, f32[2048]{0:T(1024)S(1)}, f32[2048]{0:T(1024)}) all-reduce(f32[3,512]{1,0:T(4,128)S(1)} %fusion.32, f32[2048]{0:T(1024)S(1)} %convert_reduce_fusion, f32[2048]{0:T(1024)S(1)} %copy-done.47), channel_id=1, replica_groups=mesh['dp'=8,'tensor'=4] {'dp'}, use_global_device_ids=true, to_apply=%region_18.19 | all-reduce | flops 5632 | bytes 45056 | tf_op jit(solution)/shard_map/psum | solution.py:191
  520.0 37.8 %all-reduce = (f32[2048]{0:T(1024)}, f32[2048]{0:T(1024)}) all-reduce(f32[2048]{0:T(1024)S(1)} %get-tuple-element.24, f32[2048]{0:T(1024)S(1)} %get-tuple-element.27), channel_id=1, replica_groups=mesh['dp'=8,'tensor'=4] {'dp','tensor'}, use_global_device_ids=true, to_apply=%region_13.14 | all-reduce | flops 4096 | bytes 32768 | tf_op jit(solution)/shard_map/psum | solution.py:214
  557.8 25.6 %reduce-scatter.3.cloned.1.call-done = f32[256,2048]{1,0:T(8,128)} async-done(((f32[1024,2048]{1,0:T(8,128)}), f32[256,2048]{1,0:T(8,128)}) %reduce-scatter.3.cloned.1.call-update) | async-done | bytes 2097168 | tf_op jit(solution)/shard_map/reduce_scatter | solution.py:126
  583.5 5.4 fusion.60
  588.8 961.0 %all-reduce.5.cloned.1.call-done = (f32[3,2048,512]{1,2,0:T(8,128)}, f32[512,2048]{1,0:T(8,128)}, f32[2048,2048]{1,0:T(8,128)}, f32[2048,2048]{1,0:T(8,128)}) async-done(((f32[3,2048,512]{1,2,0:T(8,128)}, f32[512,2048]{1,0:T(8,128)}, f32[2048,2048]{1,0:T(8,128)}, f32[2048,2048]{1,0:T(8,128)}), (f32[3,2048,512]{1,2,0:T(8,128)}, f32[512,2048]{1,0:T(8,128)}, f32[2048,2048]{1,0:T(8,128)}, ...) | async-done | bytes 50331664 | tf_op jit(solution)/shard_map/psum | solution.py:191
  1549.8 12.6 copy.29
  1563.0 4.8 copy.38
  1567.9 13.6 copy.39
  1583.2 6.2 copy.40
  (177 shorter events, 64.9 us)
Async XLA Ops:
  7.2 116.5 %copy-start = (bf16[512,2048]{1,0:T(8,128)(2,1)S(1)}, bf16[512,2048]{1,0:T(8,128)(2,1)}, u32[]{:S(2)}) copy-start(bf16[512,2048]{1,0:T(8,128)(2,1)} %param.17) | copy-start | bytes 6291460
  7.2 62.0 %all-gather.3.cloned.1.call-start = ((), (), s32[]{:S(2)}) async-start(), calls=%async_computation.2 | async-start | bytes 5242880 | tf_op jit(solution)/shard_map/all_gather | solution.py:87
  13.8 109.9 %all-gather.5.cloned.1.call-start = ((), (), s32[]{:S(2)}) async-start(), calls=%async_computation.4 | async-start | bytes 5242880 | tf_op jit(solution)/shard_map/all_gather | solution.py:130
  14.5 502.6 %reduce-scatter.5.cloned.1.call-start = ((), (), s32[]{:S(2)}) async-start(), calls=%async_computation.5 | async-start | bytes 10485760 | tf_op jit(solution)/shard_map/reduce_scatter | solution.py:204
  14.9 114.4 %copy-start.36 = (f32[1024,32]{0,1:T(8,128)}, f32[1024,32]{0,1:T(8,128)S(1)}, u32[]{:S(2)}) copy-start(f32[1024,32]{0,1:T(8,128)S(1)} %get-tuple-element.58) | copy-start | bytes 393220
  14.9 114.4 %copy-start.38 = (f32[1024,32]{0,1:T(8,128)}, f32[1024,32]{0,1:T(8,128)S(1)}, u32[]{:S(2)}) copy-start(f32[1024,32]{0,1:T(8,128)S(1)} %get-tuple-element.59) | copy-start | bytes 393220
  221.9 12.6 copy-start.15
  221.9 12.6 copy-start.50
  234.6 20.6 %copy-start.51 = (f32[1024,2048]{1,0:T(8,128)}, f32[1024,2048]{1,0:T(8,128)S(1)}, u32[]{:S(2)}) copy-start(f32[1024,2048]{1,0:T(8,128)S(1)} %fusion.124) | copy-start | bytes 25165828
  255.1 15.1 copy-start.13
  255.1 15.1 copy-start.25
  255.1 15.1 copy-start.27
  255.2 15.1 copy-start.29
  255.2 15.1 copy-start.31
  273.4 13.0 copy-start.1
  341.5 36.2 %copy-start.39 = (f32[1024,32]{0,1:T(8,128)S(1)}, f32[1024,32]{0,1:T(8,128)}, u32[]{:S(2)}) copy-start(f32[1024,32]{0,1:T(8,128)} %copy-done.38) | copy-start | bytes 393220
  406.9 176.5 %reduce-scatter.3.cloned.1.call-start = ((), (), s32[]{:S(2)}) async-start(), calls=%async_computation.3 | async-start | bytes 10485760 | tf_op jit(solution)/shard_map/reduce_scatter | solution.py:126
  407.0 16.7 %slice-start.4 = ((s8[8388608]{0:T(1024)(128)(4,1)}), s8[4194304]{0:T(1024)(128)(4,1)S(1)}, s32[]{:S(2)}) async-start(s8[8388608]{0:T(1024)(128)(4,1)} %bitcast.81), calls=%async_computation.11 | async-start | bytes 8388608
  441.5 1108.3 %all-reduce.5.cloned.1.call-start = ((), (), s32[]{:S(2)}) async-start(), calls=%async_computation.6 | async-start | bytes 100663296 | tf_op jit(solution)/shard_map/psum | solution.py:191
  448.5 22.1 %slice-start.6 = ((s8[8388608]{0:T(1024)(128)(4,1)}), s8[4194304]{0:T(1024)(128)(4,1)S(1)}, s32[]{:S(2)}) async-start(s8[8388608]{0:T(1024)(128)(4,1)} %bitcast.83), calls=%async_computation.13 | async-start | bytes 8388608
  458.8 11.8 slice-start.7
  483.4 33.8 %copy-start.2 = (bf16[256,2048]{1,0:T(8,128)(2,1)S(1)}, bf16[256,2048]{1,0:T(8,128)(2,1)}, u32[]{:S(2)}) copy-start(bf16[256,2048]{1,0:T(8,128)(2,1)} %param.12) | copy-start | bytes 3145732
  483.4 33.8 %copy-start.40 = (f32[2048]{0:T(1024)S(1)}, f32[2048]{0:T(1024)}, u32[]{:S(2)}) copy-start(f32[2048]{0:T(1024)} %param.13) | copy-start | bytes 24580
  483.4 33.8 %copy-start.42 = (f32[256]{0:T(256)S(1)}, f32[256]{0:T(256)}, u32[]{:S(2)}) copy-start(f32[256]{0:T(256)} %copy-done.41) | copy-start | bytes 3076
  483.4 33.8 %copy-start.44 = (f32[256]{0:T(256)S(1)}, f32[256]{0:T(256)}, u32[]{:S(2)}) copy-start(f32[256]{0:T(256)} %copy-done.43) | copy-start | bytes 3076
  483.4 100.0 %copy-start.45 = (f32[2048]{0:T(1024)S(1)}, f32[2048]{0:T(1024)}, u32[]{:S(2)}) copy-start(f32[2048]{0:T(1024)} %param.22) | copy-start | bytes 24580
  483.4 100.0 %copy-start.46 = (f32[2048]{0:T(1024)S(1)}, f32[2048]{0:T(1024)}, u32[]{:S(2)}) copy-start(f32[2048]{0:T(1024)} %param.18) | copy-start | bytes 24580
  517.2 1045.3 %copy-start.48 = (f32[2048]{0:T(1024)}, f32[2048]{0:T(1024)S(1)}, u32[]{:S(2)}) copy-start(f32[2048]{0:T(1024)S(1)} %get-tuple-element.101) | copy-start | bytes 24580
  1563.0 18.4 %slice-start = ((s8[16777216]{0:T(1024)(128)(4,1)}), s8[4194304]{0:T(1024)(128)(4,1)S(1)}, s32[]{:S(2)}) async-start(s8[16777216]{0:T(1024)(128)(4,1)} %bitcast.64), calls=%async_computation.7 | async-start | bytes 8388608
  1567.9 13.6 slice-start.1
  1567.9 13.6 slice-start.2
  1567.9 15.3 slice-start.3
  (34 other events, 181.1 us)
Sparse Core Ops, SparseCore 0:
  13.9 55.2 all-gather.2
  71.1 52.5 all-gather.4
  407.0 86.3 reduce-scatter.4
  496.3 87.0 reduce-scatter.2
  587.4 962.4 all-reduce.4
where the time goes:
time: 1610 us; the launch traced here: 1600 us
  waiting for transfers between devices  1080 us (67%)
  matrix products  339 us (21%)
  blocking collectives  66.9 us (4%)
  local copies, waits for them, and re-layouts  55.6 us (3%)
  other arithmetic  40.2 us (2%)
    psum x1, waiting for transfers between devices, shards(): lax.psum((grad_qkv_w, grad_qkv_b, grad_dense_w, grad_out_bias, grad_fc1_w...  961 us
    dot_general x2, matrix products, shards(): jnp.einsum('hqk,khd->qhd', d_scores, keys_all, preferred_element_type=jnp...  75.8 us
    dot_general x2, matrix products, shards(): jnp.einsum('hqk,qhd->khd', d_scores, q_block, preferred_element_type=jnp....  72.3 us
    all_gather x1, waiting for transfers between devices, shards(): ln_rows = lax.all_gather(ln_local, 'tensor', axis=0, tiled=True)  52.2 us
    unnamed x127, local copies, waits for them, and re-layouts  43.2 us
    all_gather x1, waiting for transfers between devices, shards(): cot_rows = lax.all_gather(cotangent, 'tensor', axis=0, tiled=True)  39.8 us
    psum x1, blocking collectives, shards(): lax.psum((local_gain, local_shift), ('dp', 'tensor'))  37.8 us
  transfers between devices with their start and end apart: 5, of which 4 were waited for; matrix products, arithmetic and copies ran while one was open for 7% of the time, Pallas kernels for 0%

commit v1 on v0

--- a/solution.py
+++ b/solution.py
@@ -10,6 +10,14 @@
 gelu_scale = math.sqrt(2.0 / math.pi)
 gelu_cubic = 0.044715
 masked_value = -1e30
+
+
+def link_things(frame_in, dim_k):
+    frame_in = jnp.moveaxis(frame_in, 0, dim_k)
+    formed = frame_in.shape
+    return frame_in.reshape(
+        *formed[:dim_k], formed[dim_k] * formed[dim_k + 1], *formed[dim_k + 2 :]
+    )
 
 
 def rope_tables(length):
@@ -127,7 +135,30 @@
     block_output = (block_input.astype(jnp.float32) + summed + dense_bias + fc2_bias).astype(
         jnp.bfloat16
     )
-    cot_rows = lax.all_gather(cotangent, "tensor", axis=0, tiled=True)
+    count_all = lax.psum(1, axis_name="tensor")
+    runs = []
+    d = 0
+    while d < count_all:
+        runs.append((d, (d + 1) % count_all))
+        d += 1
+    items = []
+    for ii, w in runs:
+        items.append((w, ii))
+    tmp, plain = ([], [])
+    t = 0
+    while t < count_all - 1:
+        if t % 2 == 0:
+            tmp.append(lax.ppermute(tmp[-1] if tmp else cotangent, axis_name="tensor", perm=runs))
+        else:
+            plain.append(
+                lax.ppermute(plain[-1] if plain else cotangent, perm=items, axis_name="tensor")
+            )
+        t += 1
+    passed = jnp.stack([*tmp[::-1], cotangent, *plain])
+    w2 = lax.axis_index("tensor")
+    v1 = w2 - len(tmp)
+    passed = passed[(jnp.arange(count_all) - v1) % count_all]
+    cot_rows = link_things(passed, 0)
     grad_out_bias = jnp.sum(cot_rows.astype(jnp.float32), axis=0)
     grad_fc2_w = jnp.dot(act_b.T, cot_rows, preferred_element_type=jnp.float32)
     d_pre = jnp.dot(cot_rows, fc2_weight.T, preferred_element_type=jnp.float32) * act_slope

time: 1610 us -> 1620 us (level)
    ppermute x0 -> x3, waiting for transfers between devices: none -> 98.5 us  [the longest x2 60 us: shards(): lax.ppermute(tmp[-1] if tmp else cotangent, axis_name='tensor', perm=runs)]
    all_gather x1, waiting for transfers between devices: 52.2 us -> 0.01 us  [shards(): ln_rows = lax.all_gather(ln_local, 'tensor', axis=0, tiled=True)]
    all_gather x1 -> x0, waiting for transfers between devices: 39.8 us -> none  [shards(): cot_rows = lax.all_gather(cotangent, 'tensor', axis=0, tiled=True)]
    unnamed x127 -> x111, local copies, waits for them, and re-layouts: 43.2 us -> 42.8 us
  transfers between devices with their start and end apart: 5 -> 7, of which waited for: 4 -> 5; matrix products, arithmetic and copies ran while one was open for 7% -> 7% of each run, Pallas kernels for 0% -> 0%
where the time goes in v1:
time: 1620 us; the launch traced here: 1610 us
  waiting for transfers between devices  1080 us (67%)
  matrix products  338 us (21%)
  blocking collectives  67.5 us (4%)
  local copies, waits for them, and re-layouts  58.1 us (4%)
  other arithmetic  45.1 us (3%)
    psum x1, waiting for transfers between devices, shards(): lax.psum((grad_qkv_w, grad_qkv_b, grad_dense_w, grad_out_bias, grad_fc1_w...  961 us
    dot_general x2, matrix products, shards(): jnp.einsum('hqk,khd->qhd', d_scores, keys_all, preferred_element_type=jnp...  75.7 us
    dot_general x2, matrix products, shards(): jnp.einsum('hqk,qhd->khd', d_scores, q_block, preferred_element_type=jnp....  72.2 us
    ppermute x2, waiting for transfers between devices, shards(): lax.ppermute(tmp[-1] if tmp else cotangent, axis_name='tensor', perm=runs)  60 us
    unnamed x111, local copies, waits for them, and re-layouts  42.8 us
    psum x1, blocking collectives, shards(): lax.psum((local_gain, local_shift), ('dp', 'tensor'))  38.5 us
    ppermute x1, waiting for transfers between devices, shards(): lax.ppermute(plain[-1] if plain else cotangent, perm=items, axis_name='te...  38.4 us
  transfers between devices with their start and end apart: 7, of which 5 were waited for; matrix products, arithmetic and copies ran while one was open for 7% of the time, Pallas kernels for 0%

profile of v1, /device:TPU:0, one launch (start us, length us, event | category | flops | bytes accessed | tf_op | source)
XLA Modules:
  0.0 1613.1 jit_solution(11682815540436451666)
XLA Ops:
  17.9 35.4 %collective-permute-done = bf16[256,2048]{1,0:T(8,128)(2,1)S(1)} collective-permute-done((bf16[256,2048]{1,0:T(8,128)(2,1)}, bf16[256,2048]{1,0:T(8,128)(2,1)S(1)}, u32[]{:S(2)}, u32[]{:S(2)}) %collective-permute-start) | collective-permute-done | bytes 1048608 | tf_op jit(solution)/shard_map/ppermute | solution.py:151
  56.8 38.4 %collective-permute-done.2 = bf16[256,2048]{1,0:T(8,128)(2,1)} collective-permute-done((bf16[256,2048]{1,0:T(8,128)(2,1)}, bf16[256,2048]{1,0:T(8,128)(2,1)}, u32[]{:S(2)}, u32[]{:S(2)}) %collective-permute-start.2) | collective-permute-done | bytes 1048608 | tf_op jit(solution)/shard_map/ppermute | solution.py:154
  95.3 24.6 %collective-permute-done.1 = bf16[256,2048]{1,0:T(8,128)(2,1)} collective-permute-done((bf16[256,2048]{1,0:T(8,128)(2,1)S(1)}, bf16[256,2048]{1,0:T(8,128)(2,1)}, u32[]{:S(2)}, u32[]{:S(2)}) %collective-permute-start.1) | collective-permute-done | bytes 1048608 | tf_op jit(solution)/shard_map/ppermute | solution.py:151
  124.0 5.0 gather_fusion
  134.7 10.4 add_bitcast_fusion
  155.9 8.5 fusion.127
  164.4 37.9 %fusion.78 = f32[512,8,64]{0,2,1:T(8,128)} fusion(f32[8,512,1024]{2,1,0:T(8,128)} %fusion.127, bf16[1024,8,32]{0,2,1:T(8,128)(2,1)} %copy-done.19, bf16[1024,8,32]{0,2,1:T(8,128)(2,1)} %copy-done.25, f32[8,512,1024]{2,1,0:T(8,128)} %copy-done.3, f32[8,512]{1,0:T(8,128)S(1)} %log_add_fusion.1, pred[512,1024]{1,0:T(8,128)(4,1)} %iota_compare_fusion.2), kind=kOutput, calls=%fused_computation.94 | convolution fusion | flops 585110528 | bytes 36192256 | tf_op jit(solution)/shard_map/hqk,khd->qhd/dot_general | solution.py:191
  202.3 36.2 %fusion.11 = f32[8,64,1024]{2,1,0:T(8,128)} fusion(f32[8,512,1024]{2,1,0:T(8,128)} %fusion.127, bf16[1024,8,32]{0,2,1:T(8,128)(2,1)} %copy-done.23, bf16[1024,8,32]{0,2,1:T(8,128)(2,1)} %copy-done.21, f32[8,512,1024]{2,1,0:T(8,128)} %copy-done.3, f32[8,512]{1,0:T(8,128)S(1)} %log_add_fusion.1, pred[512,1024]{1,0:T(8,128)(4,1)} %iota_compare_fusion.2), kind=kOutput, calls=%fused_computation.19 | convolution fusion | flops 584061952 | bytes 71335936 | tf_op jit(solution)/shard_map/hqk,qhd->khd/dot_general | solution.py:193
  238.5 12.6 fusion.126
  251.1 20.6 %fusion.125 = (f32[2048]{0:T(1024)}, bf16[1024,2048]{1,0:T(8,128)(2,1)}) fusion(f32[1024,2048]{1,0:T(8,128)S(1)} %fusion.126, f32[2048]{0:T(1024)S(1)} %copy-done.42, bf16[1024,2048]{1,0:T(8,128)(2,1)S(1)} %bitcast.75, bf16[2048,2048]{1,0:T(8,128)(2,1)} %param.21), kind=kOutput, calls=%fused_computation.161 | convolution fusion | flops 8633972736 | bytes 25182208 | tf_op jit(solution)/shard_map/dot_general | solution.py:164
  271.7 15.1 fusion.68
  294.3 8.5 fusion.128
  307.5 9.8 fusion.72
  320.2 37.8 %fusion.75 = f32[512,8,64]{0,2,1:T(8,128)} fusion(f32[8,512,1024]{2,1,0:T(8,128)} %fusion.128, bf16[1024,8,32]{0,2,1:T(8,128)(2,1)} %copy-done.19, bf16[1024,8,32]{0,2,1:T(8,128)(2,1)} %copy-done.25, f32[8,512,1024]{2,1,0:T(8,128)} %copy-done.1, f32[8,512]{1,0:T(8,128)S(1)} %log_add_fusion, pred[512,1024]{1,0:T(8,128)(4,1)} %iota_compare_fusion.1), kind=kOutput, calls=%fused_computation.93 | convolution fusion | flops 585110528 | bytes 36192256 | tf_op jit(solution)/shard_map/hqk,khd->qhd/dot_general | solution.py:191
  358.0 36.0 %add_bitcast_fusion.1 = f32[1024,8,64]{0,2,1:T(8,128)} fusion(f32[8,64,1024]{2,1,0:T(8,128)} %fusion.11, f32[8,512,1024]{2,1,0:T(8,128)} %fusion.128, bf16[1024,8,32]{0,2,1:T(8,128)(2,1)} %copy-done.21, bf16[1024,8,32]{0,2,1:T(8,128)(2,1)} %copy-done.23, f32[8,512,1024]{2,1,0:T(8,128)} %copy-done.1, f32[8,512]{1,0:T(8,128)S(1)} %log_add_fusion, ...), kind=kOutput, calls=%fused_computation.83 | convolution fusion | flops 584586240 | bytes 39337984 | tf_op jit(solution)/shard_map/hqk,qhd->khd/dot_general | solution.py:193
  409.3 13.9 bitcast_add_fusion
  423.3 8.3 fusion.87
  431.6 8.1 fusion.90
  439.9 12.1 fusion.120
  452.0 5.6 convolution_add_fusion
  457.7 6.8 fusion.129
  464.6 10.3 convolution_bitcast_fusion
  474.8 11.8 fusion.66
  486.7 12.7 fusion.119
  505.8 29.0 %all-reduce.1 = (f32[3,512]{1,0:T(4,128)}, f32[2048]{0:T(1024)S(1)}, f32[2048]{0:T(1024)}) all-reduce(f32[3,512]{1,0:T(4,128)S(1)} %fusion.32, f32[2048]{0:T(1024)S(1)} %convert_reduce_fusion, f32[2048]{0:T(1024)S(1)} %copy-done.38), channel_id=1, replica_groups=mesh['dp'=8,'tensor'=4] {'dp'}, use_global_device_ids=true, to_apply=%region_18.19 | all-reduce | flops 5632 | bytes 45056 | tf_op jit(solution)/shard_map/psum | solution.py:222
  537.4 38.5 %all-reduce = (f32[2048]{0:T(1024)}, f32[2048]{0:T(1024)}) all-reduce(f32[2048]{0:T(1024)S(1)} %get-tuple-element.24, f32[2048]{0:T(1024)S(1)} %get-tuple-element.27), channel_id=1, replica_groups=mesh['dp'=8,'tensor'=4] {'dp','tensor'}, use_global_device_ids=true, to_apply=%region_13.14 | all-reduce | flops 4096 | bytes 32768 | tf_op jit(solution)/shard_map/psum | solution.py:245
  575.9 24.6 %reduce-scatter.3.cloned.1.call-done = f32[256,2048]{1,0:T(8,128)} async-done(((f32[1024,2048]{1,0:T(8,128)}), f32[256,2048]{1,0:T(8,128)}) %reduce-scatter.3.cloned.1.call-update) | async-done | bytes 2097168 | tf_op jit(solution)/shard_map/reduce_scatter | solution.py:134
  600.5 5.4 fusion.60
  605.8 961.0 %all-reduce.5.cloned.1.call-done = (f32[3,2048,512]{1,2,0:T(8,128)}, f32[512,2048]{1,0:T(8,128)}, f32[2048,2048]{1,0:T(8,128)}, f32[2048,2048]{1,0:T(8,128)}) async-done(((f32[3,2048,512]{1,2,0:T(8,128)}, f32[512,2048]{1,0:T(8,128)}, f32[2048,2048]{1,0:T(8,128)}, f32[2048,2048]{1,0:T(8,128)}), (f32[3,2048,512]{1,2,0:T(8,128)}, f32[512,2048]{1,0:T(8,128)}, f32[2048,2048]{1,0:T(8,128)}, ...) | async-done | bytes 50331664 | tf_op jit(solution)/shard_map/psum | solution.py:222
  1566.8 12.6 copy.29
  1584.9 13.6 copy.39
  1600.2 6.2 copy.40
  (168 shorter events, 81.2 us)
Async XLA Ops:
  7.2 121.8 %copy-start = (bf16[512,2048]{1,0:T(8,128)(2,1)S(1)}, bf16[512,2048]{1,0:T(8,128)(2,1)}, u32[]{:S(2)}) copy-start(bf16[512,2048]{1,0:T(8,128)(2,1)} %param.17) | copy-start | bytes 6291460
  7.2 127.5 %all-gather.2.cloned.1.call-start = ((), (), s32[]{:S(2)}) async-start(), calls=%async_computation.2 | async-start | bytes 5242880 | tf_op jit(solution)/shard_map/all_gather | solution.py:95
  13.8 521.0 %reduce-scatter.5.cloned.1.call-start = ((), (), s32[]{:S(2)}) async-start(), calls=%async_computation.4 | async-start | bytes 10485760 | tf_op jit(solution)/shard_map/reduce_scatter | solution.py:235
  13.8 39.4 %collective-permute-start = (bf16[256,2048]{1,0:T(8,128)(2,1)}, bf16[256,2048]{1,0:T(8,128)(2,1)S(1)}, u32[]{:S(2)}, u32[]{:S(2)}) collective-permute-start(bf16[256,2048]{1,0:T(8,128)(2,1)} %param.23), channel_id=1, source_target_pairs={{0,1},{1,2},{2,3},{3,0},{4,5},{5,6},{6,7},{7,4},{8,9},{9,10},{10,1... | collective-permute-start | bytes 3145736 | tf_op jit(solution)/shard_map/ppermute | solution.py:151
  16.8 78.4 %collective-permute-start.2 = (bf16[256,2048]{1,0:T(8,128)(2,1)}, bf16[256,2048]{1,0:T(8,128)(2,1)}, u32[]{:S(2)}, u32[]{:S(2)}) collective-permute-start(bf16[256,2048]{1,0:T(8,128)(2,1)} %param.23), channel_id=1, source_target_pairs={{1,0},{2,1},{3,2},{0,3},{5,4},{6,5},{7,6},{4,7},{9,8},{10,9},{11,1... | collective-permute-start | bytes 3145736 | tf_op jit(solution)/shard_map/ppermute | solution.py:154
  53.2 66.7 %collective-permute-start.1 = (bf16[256,2048]{1,0:T(8,128)(2,1)S(1)}, bf16[256,2048]{1,0:T(8,128)(2,1)}, u32[]{:S(2)}, u32[]{:S(2)}) collective-permute-start(bf16[256,2048]{1,0:T(8,128)(2,1)S(1)} %collective-permute-done), channel_id=1, source_target_pairs={{0,1},{1,2},{2,3},{3,0},{4,5},{5,6},{6,7},{7,4},{8,9},{9,10},{10,1... | collective-permute-start | bytes 3145736 | tf_op jit(solution)/shard_map/ppermute | solution.py:151
  54.7 91.2 %copy-start.27 = (f32[1024,32]{0,1:T(8,128)}, f32[1024,32]{0,1:T(8,128)S(1)}, u32[]{:S(2)}) copy-start(f32[1024,32]{0,1:T(8,128)S(1)} %get-tuple-element.58) | copy-start | bytes 393220
  54.7 91.2 %copy-start.29 = (f32[1024,32]{0,1:T(8,128)}, f32[1024,32]{0,1:T(8,128)S(1)}, u32[]{:S(2)}) copy-start(f32[1024,32]{0,1:T(8,128)S(1)} %get-tuple-element.59) | copy-start | bytes 393220
  238.5 12.6 copy-start.42
  251.1 20.6 %copy-start.43 = (f32[1024,2048]{1,0:T(8,128)}, f32[1024,2048]{1,0:T(8,128)S(1)}, u32[]{:S(2)}) copy-start(f32[1024,2048]{1,0:T(8,128)S(1)} %fusion.126) | copy-start | bytes 25165828
  271.7 15.1 copy-start.11
  271.7 15.1 copy-start.20
  271.7 15.1 copy-start.22
  271.7 15.1 copy-start.24
  271.7 15.1 copy-start.26
  289.9 13.0 copy-start.1
  358.0 36.0 %copy-start.30 = (f32[1024,32]{0,1:T(8,128)S(1)}, f32[1024,32]{0,1:T(8,128)}, u32[]{:S(2)}) copy-start(f32[1024,32]{0,1:T(8,128)} %copy-done.29) | copy-start | bytes 393220
  423.2 177.2 %reduce-scatter.3.cloned.1.call-start = ((), (), s32[]{:S(2)}) async-start(), calls=%async_computation.3 | async-start | bytes 10485760 | tf_op jit(solution)/shard_map/reduce_scatter | solution.py:134
  423.3 16.6 %slice-start.4 = ((s8[8388608]{0:T(1024)(128)(4,1)}), s8[4194304]{0:T(1024)(128)(4,1)S(1)}, s32[]{:S(2)}) async-start(s8[8388608]{0:T(1024)(128)(4,1)} %bitcast.94), calls=%async_computation.10 | async-start | bytes 8388608
  457.6 1109.2 %all-reduce.5.cloned.1.call-start = ((), (), s32[]{:S(2)}) async-start(), calls=%async_computation.5 | async-start | bytes 100663296 | tf_op jit(solution)/shard_map/psum | solution.py:222
  464.6 22.1 %slice-start.6 = ((s8[8388608]{0:T(1024)(128)(4,1)}), s8[4194304]{0:T(1024)(128)(4,1)S(1)}, s32[]{:S(2)}) async-start(s8[8388608]{0:T(1024)(128)(4,1)} %bitcast.96), calls=%async_computation.12 | async-start | bytes 8388608
  499.4 35.4 %copy-start.2 = (bf16[256,2048]{1,0:T(8,128)(2,1)S(1)}, bf16[256,2048]{1,0:T(8,128)(2,1)}, u32[]{:S(2)}) copy-start(bf16[256,2048]{1,0:T(8,128)(2,1)} %param.12) | copy-start | bytes 3145732
  499.4 35.3 %copy-start.31 = (f32[2048]{0:T(1024)S(1)}, f32[2048]{0:T(1024)}, u32[]{:S(2)}) copy-start(f32[2048]{0:T(1024)} %param.13) | copy-start | bytes 24580
  499.4 35.3 %copy-start.33 = (f32[256]{0:T(256)S(1)}, f32[256]{0:T(256)}, u32[]{:S(2)}) copy-start(f32[256]{0:T(256)} %copy-done.32) | copy-start | bytes 3076
  499.5 35.3 %copy-start.35 = (f32[256]{0:T(256)S(1)}, f32[256]{0:T(256)}, u32[]{:S(2)}) copy-start(f32[256]{0:T(256)} %copy-done.34) | copy-start | bytes 3076
  499.5 101.0 %copy-start.36 = (f32[2048]{0:T(1024)S(1)}, f32[2048]{0:T(1024)}, u32[]{:S(2)}) copy-start(f32[2048]{0:T(1024)} %param.22) | copy-start | bytes 24580
  499.5 101.0 %copy-start.37 = (f32[2048]{0:T(1024)S(1)}, f32[2048]{0:T(1024)}, u32[]{:S(2)}) copy-start(f32[2048]{0:T(1024)} %param.18) | copy-start | bytes 24580
  534.8 1044.7 %copy-start.39 = (f32[2048]{0:T(1024)}, f32[2048]{0:T(1024)S(1)}, u32[]{:S(2)}) copy-start(f32[2048]{0:T(1024)S(1)} %get-tuple-element.101) | copy-start | bytes 24580
  1580.0 18.4 %slice-start = ((s8[16777216]{0:T(1024)(128)(4,1)}), s8[4194304]{0:T(1024)(128)(4,1)S(1)}, s32[]{:S(2)}) async-start(s8[16777216]{0:T(1024)(128)(4,1)} %bitcast.71), calls=%async_computation.6 | async-start | bytes 8388608
  1584.9 13.6 slice-start.1
  1584.9 13.6 slice-start.2
  1584.9 15.3 slice-start.3
  (28 other events, 156.4 us)
Sparse Core Ops, SparseCore 0:
  13.9 88.6 all-gather.1
  423.4 86.8 reduce-scatter.4
  513.3 87.0 reduce-scatter.2
  604.4 962.4 all-reduce.4
